TPU v7x, 32 devices: a whole 2x2x4 slice. The times are simulated.
32 devices in a mesh: wire: 16 (over z, y, x), col: 2 (over core).
Axes of the slice: x: 2, y: 2, z: 4, core: 2. Of those that a mesh axis runs over, the one named last changes fastest.
Arguments:
- hamiltonian: bfloat16 [256, 3, 128, 128], P('wire')
- offsets: int32 [256, 3], P('wire'), may hold values from -2 to 2, as said below
- phase_left: bfloat16 [32768, 2048], P('wire'), may hold values from -0.125 to 0.125
- phase_right: bfloat16 [32768, 2048], P('wire'), may hold values from -0.03125 to 0.03125
- orbitals: bfloat16 [32768, 512], P('wire', 'col'), may hold values from -6 to 6
Outputs:
- gradient: float32 [32768, 512], P('wire', 'col')
Inputs may be any that keep to these rules, and one draw needn't show every extreme that they name: `offsets`: slot 0 of every row block has offset 0.
All inputs are finite; a program needn't handle non-finite values.
Results may differ from a plain program's by a relative error of at most 0.0017.
Values may be sent and summed in bfloat16 or wider, within the bound.
No kernel may reach another device: no remote copies, remote signals or barrier semaphores. Data moves between devices by JAX's collectives and lax.ppermute only.
A program may use at most 128 MiB of HBM per device.

v0:
```python
import jax
import jax.numpy as jnp
from jax import lax
from jax.sharding import PartitionSpec as P

REACH = 2


def padded_2(shard, sides, width):
    for axis, dim in sides:
        devices, length = (lax.axis_size(axis), shard.shape[dim])
        up = [(i, (i + 1) % devices) for i in range(devices)]
        down = [(j, i) for i, j in up]
        last = lax.slice_in_dim(shard, length - width, length, axis=dim)
        leading = lax.slice_in_dim(shard, 0, width, axis=dim)
        before = lax.ppermute(last, axis, up)
        after = lax.ppermute(leading, axis, down)
        shard = jnp.concatenate([before, shard, after], axis=dim)
    return shard


def body(hamiltonian, offsets, phase_left, phase_right, orbitals):
    local_blocks = hamiltonian.shape[0]
    block_size = hamiltonian.shape[2]
    local_rows = orbitals.shape[0]
    total_rows = local_rows * lax.axis_size("wire")
    padded = padded_2(orbitals, (("wire", 0),), REACH * block_size)
    tiles = padded.reshape(local_blocks + 2 * REACH, block_size, orbitals.shape[1])
    picks = jnp.arange(local_blocks, dtype=jnp.int32)[:, None] + offsets + REACH
    picked = jnp.take(tiles, picks, axis=0)
    band = jnp.einsum(
        "jsab,jsbm->jam", hamiltonian, picked, preferred_element_type=jnp.float32
    ).reshape(local_rows, orbitals.shape[1])
    full = lax.all_gather(orbitals, "col", axis=1, tiled=True)
    coupling_part = jnp.dot(phase_right.T, orbitals, preferred_element_type=jnp.float32)
    intersection_part = jnp.dot(full.T, orbitals, preferred_element_type=jnp.float32)
    coupling, intersection = lax.psum((coupling_part, intersection_part), "wire")
    coupling_low = coupling.astype(jnp.bfloat16)
    image = band + jnp.dot(phase_left, coupling_low, preferred_element_type=jnp.float32)
    full_wide = full.astype(jnp.float32)
    cross_part = jnp.dot(full_wide.T, image, precision=lax.Precision.HIGHEST)
    cross = lax.psum(cross_part, "wire")
    intersection_scaled = intersection / total_rows
    cross_scaled = cross / total_rows
    partial_terms = jnp.dot(image, intersection_scaled.T, precision=lax.Precision.HIGHEST)
    mixed = lax.psum_scatter(partial_terms, "col", scatter_dimension=1, tiled=True)
    gradient = (
        2.0 * image - mixed - jnp.dot(full_wide, cross_scaled, precision=lax.Precision.HIGHEST)
    )
    return gradient


def solution(mesh):
    return jax.shard_map(
        body,
        mesh=mesh,
        in_specs=(
            P("wire", None, None, None),
            P("wire", None),
            P("wire", None),
            P("wire", None),
            P("wire", "col"),
        ),
        out_specs=P("wire", "col"),
        check_vma=False,
    )
```

profile of v0, /device:TPU:0, one launch (start us, length us, event | category | flops | bytes accessed | tf_op | source)
XLA Modules:
  0.0 296.8 jit_solution(2120622516897004435)
XLA Ops:
  6.5 0.0 copy-start
  6.5 0.0 all-gather.2.cloned.1.call-start
  6.5 0.7 all-gather.2.cloned.1.call-update
  7.3 0.0 all-reduce.4.cloned.1.call-start
  7.3 1.0 fusion.15
  8.3 3.0 %collective-permute-start = (bf16[256,256]{1,0:T(8,128)(2,1)S(1)}, bf16[256,256]{1,0:T(8,128)(2,1)S(1)}, u32[]{:S(2)}, u32[]{:S(2)}) collective-permute-start(bf16[256,256]{1,0:T(8,128)(2,1)S(1)} %get-tuple-element.7), channel_id=1, source_target_pairs={{0,2},{2,4},{4,6},{6,8},{8,10},{10,12},{12,14},{14,16},{16,18},{18... | collective-permute-start | bytes 393224 | tf_op jit(solution)/shard_map/ppermute | solution.py:16
  11.3 4.1 %collective-permute-start.1 = (bf16[256,256]{1,0:T(8,128)(2,1)S(1)}, bf16[256,256]{1,0:T(8,128)(2,1)S(1)}, u32[]{:S(2)}, u32[]{:S(2)}) collective-permute-start(bf16[256,256]{1,0:T(8,128)(2,1)S(1)} %get-tuple-element.8), channel_id=1, source_target_pairs={{2,0},{4,2},{6,4},{8,6},{10,8},{12,10},{14,12},{16,14},{18,16},{20... | collective-permute-start | bytes 393224 | tf_op jit(solution)/shard_map/ppermute | solution.py:17
  15.4 7.9 %fusion.16 = f32[2048,256]{1,0:T(8,128)} fusion(bf16[2048,2048]{1,0:T(8,128)(2,1)} %param.8, bf16[2048,256]{1,0:T(8,128)(2,1)} %param.9), kind=kOutput, calls=%fused_computation.24 | convolution fusion | flops 2147483648 | bytes 11534336 | tf_op jit(solution)/shard_map/dot_general | solution.py:35
  23.3 0.0 copy-start.4
  23.3 99.8 %all-reduce.5 = bf16[2048,256]{1,0:T(8,128)(2,1)} all-reduce(f32[2048,256]{1,0:T(8,128)} %fusion.16), channel_id=1, replica_groups=mesh['wire'=16,'col'=2] {'wire'}, use_global_device_ids=true, to_apply=%region_0.1 | all-reduce | flops 524288 | bytes 3145728 | tf_op jit(solution)/shard_map/psum | solution.py:37
  123.1 0.0 copy-done.4
  123.1 0.1 copy.11
  123.2 0.1 copy.12
  123.3 0.1 reshape.15
  123.4 0.0 collective-permute-done
  123.4 0.0 collective-permute-done.1
  123.4 1.3 pad_maximum_fusion
  124.7 2.5 gather_fusion
  127.2 0.0 copy-done
  127.2 4.0 %fusion = f32[16,256,128,1]{1,2,3,0:T(8,128)} fusion(bf16[16,3,128,128]{3,2,1,0:T(8,128)(2,1)S(1)} %copy-done, bf16[16,3,128,256]{3,2,1,0:T(8,128)(2,1)} %bitcast.30, pred[16,3]{1,0:T(8,128)(4,1)S(1)} %copy.11), kind=kOutput, calls=%fused_computation.1 | convolution fusion | flops 404226048 | bytes 6815792 | tf_op jit(solution)/shard_map/jsab,jsbm->jam/dot_general | solution.py:31
  131.3 2.9 copy.13
  134.2 0.0 copy-start.2
  134.2 8.1 %fusion.4 = f32[2048,256]{0,1:T(8,128)} fusion(f32[2048,256]{0,1:T(8,128)} %copy.13, bf16[2048,2048]{1,0:T(8,128)(2,1)} %param.7, bf16[2048,256]{1,0:T(8,128)(2,1)} %all-reduce.5), kind=kOutput, calls=%fused_computation.7 | convolution fusion | flops 2148007936 | bytes 13631488 | tf_op jit(solution)/shard_map/dot_general | solution.py:39
  142.3 0.0 all-gather.2.cloned.1.call-done
  142.3 0.0 copy-done.2
  142.3 0.0 copy-start.1
  142.3 3.3 %fusion.17 = f32[512,256]{1,0:T(8,128)} fusion(bf16[2048,512]{1,0:T(8,128)(2,1)} %all-gather.2.cloned.1.call-done, bf16[2048,256]{1,0:T(8,128)(2,1)S(1)} %copy-done.2), kind=kOutput, calls=%fused_computation.25 | convolution fusion | flops 536870912 | bytes 3670016 | tf_op jit(solution)/shard_map/dot_general | solution.py:36
  145.6 0.0 copy-done.1
  145.6 4.9 %convolution_bitcast_fusion.2 = f32[512,256]{1,0:T(8,128)} fusion(f32[2048,256]{0,1:T(8,128)} %fusion.4, bf16[2048,512]{1,0:T(8,128)(2,1)S(1)} %copy-done.1), kind=kOutput, calls=%fused_computation.10 | convolution fusion | flops 3221225472 | bytes 4718592 | tf_op jit(solution)/shard_map/dot_general | solution.py:41
  150.4 0.0 all-reduce.4.cloned.1.call-update
  150.5 0.2 reduce-scatter.2.cloned.1.call-start
  150.7 110.5 %all-reduce.4.cloned.1.call-done = (f32[512,256]{1,0:T(8,128)}, f32[512,256]{1,0:T(8,128)}) async-done(((f32[512,256]{1,0:T(8,128)}, f32[512,256]{1,0:T(8,128)}), (f32[512,256]{1,0:T(8,128)}, f32[512,256]{1,0:T(8,128)})) %all-reduce.4.cloned.1.call-update) | async-done | bytes 1048592 | tf_op jit(solution)/shard_map/psum | solution.py:37
  261.2 7.2 %fusion.8 = f32[2048,512]{0,1:T(8,128)} fusion(f32[2048,256]{0,1:T(8,128)} %fusion.4, f32[512,256]{1,0:T(8,128)} %get-tuple-element.5), kind=kOutput, calls=%fused_computation.13 | convolution fusion | flops 3221356544 | bytes 6815744 | tf_op jit(solution)/shard_map/dot_general | solution.py:45
  268.4 0.0 copy-start.3
  268.4 0.0 reduce-scatter.2.cloned.1.call-update
  268.4 11.3 %reduce-scatter.2.cloned.1.call-done = f32[2048,256]{0,1:T(8,128)} async-done(((f32[2048,512]{0,1:T(8,128)}), f32[2048,256]{0,1:T(8,128)}) %reduce-scatter.2.cloned.1.call-update) | async-done | bytes 2097168 | tf_op jit(solution)/shard_map/reduce_scatter | solution.py:46
  279.7 0.0 copy-done.3
  279.7 7.7 %fusion.3 = f32[2048,256]{0,1:T(8,128)} fusion(bf16[2048,512]{1,0:T(8,128)(2,1)} %all-gather.2.cloned.1.call-done, f32[2048,256]{0,1:T(8,128)} %reduce-scatter.2.cloned.1.call-done, f32[2048,256]{0,1:T(8,128)} %fusion.4, f32[512,256]{1,0:T(8,128)S(1)} %copy-done.3), kind=kOutput, calls=%fused_computation.6 | convolution fusion | flops 3222929408 | bytes 8912896 | tf_op jit(solution)/shard_map/dot_general | solution.py:48
  287.3 2.9 copy.15
  (3 shorter events, 0.0 us)
Async XLA Ops:
  6.5 120.7 %copy-start = (bf16[16,3,128,128]{3,2,1,0:T(8,128)(2,1)S(1)}, bf16[16,3,128,128]{3,2,1,0:T(8,128)(2,1)}, u32[]{:S(2)}) copy-start(bf16[16,3,128,128]{3,2,1,0:T(8,128)(2,1)} %param.5) | copy-start | bytes 4718596
  6.5 135.7 %all-gather.2.cloned.1.call-start = ((), (), s32[]{:S(2)}) async-start(), calls=%async_computation.1 | async-start | bytes 3145728 | tf_op jit(solution)/shard_map/all_gather | solution.py:34
  7.3 253.9 %all-reduce.4.cloned.1.call-start = ((), (), s32[]{:S(2)}) async-start(), calls=%async_computation.3 | async-start | bytes 2097152 | tf_op jit(solution)/shard_map/psum | solution.py:37
  8.3 115.1 %collective-permute-start = (bf16[256,256]{1,0:T(8,128)(2,1)S(1)}, bf16[256,256]{1,0:T(8,128)(2,1)S(1)}, u32[]{:S(2)}, u32[]{:S(2)}) collective-permute-start(bf16[256,256]{1,0:T(8,128)(2,1)S(1)} %get-tuple-element.7), channel_id=1, source_target_pairs={{0,2},{2,4},{4,6},{6,8},{8,10},{10,12},{12,14},{14,16},{16,18},{18... | collective-permute-start | bytes 393224 | tf_op jit(solution)/shard_map/ppermute | solution.py:16
  11.3 112.1 %collective-permute-start.1 = (bf16[256,256]{1,0:T(8,128)(2,1)S(1)}, bf16[256,256]{1,0:T(8,128)(2,1)S(1)}, u32[]{:S(2)}, u32[]{:S(2)}) collective-permute-start(bf16[256,256]{1,0:T(8,128)(2,1)S(1)} %get-tuple-element.8), channel_id=1, source_target_pairs={{2,0},{4,2},{6,4},{8,6},{10,8},{12,10},{14,12},{16,14},{18,16},{20... | collective-permute-start | bytes 393224 | tf_op jit(solution)/shard_map/ppermute | solution.py:17
  23.3 99.8 %copy-start.4 = (s32[16,3]{0,1:T(4,128)S(1)}, s32[16,3]{0,1:T(4,128)}, u32[]{:S(2)}) copy-start(s32[16,3]{0,1:T(4,128)} %param.6) | copy-start | bytes 580
  134.2 8.1 %copy-start.2 = (bf16[2048,256]{1,0:T(8,128)(2,1)S(1)}, bf16[2048,256]{1,0:T(8,128)(2,1)}, u32[]{:S(2)}) copy-start(bf16[2048,256]{1,0:T(8,128)(2,1)} %param.9) | copy-start | bytes 3145732
  142.3 3.3 %copy-start.1 = (bf16[2048,512]{1,0:T(8,128)(2,1)S(1)}, bf16[2048,512]{1,0:T(8,128)(2,1)}, u32[]{:S(2)}) copy-start(bf16[2048,512]{1,0:T(8,128)(2,1)} %all-gather.2.cloned.1.call-done) | copy-start | bytes 6291460
  150.5 129.2 %reduce-scatter.2.cloned.1.call-start = ((), (), s32[]{:S(2)}) async-start(), calls=%async_computation.2 | async-start | bytes 6291456 | tf_op jit(solution)/shard_map/reduce_scatter | solution.py:46
  268.4 11.3 %copy-start.3 = (f32[512,256]{1,0:T(8,128)S(1)}, f32[512,256]{1,0:T(8,128)}, u32[]{:S(2)}) copy-start(f32[512,256]{1,0:T(8,128)} %get-tuple-element.6) | copy-start | bytes 1572868
Sparse Core Ops, SparseCore 0:
  8.9 12.8 all-gather.1
  150.6 110.5 all-reduce.3
  268.5 11.1 reduce-scatter.1
where the time goes:
time: 297 us
  waiting for transfers between devices  123 us (41%)
  blocking collectives  99.8 us (34%)
  matrix products  43.1 us (15%)
  between operations  13.2 us (4%)
  local copies, waits for them, and re-layouts  9.57 us (3%)
  starting transfers between devices  7.34 us (2%)
    psum x1, waiting for transfers between devices, body(): lax.psum((coupling_part, intersection_part), 'wire')  110 us
    psum x1, blocking collectives, body(): lax.psum((coupling_part, intersection_part), 'wire')  99.8 us
    reduce_scatter x1, waiting for transfers between devices, body(): lax.psum_scatter(partial_terms, 'col', scatter_dimension=1, tiled=True)  11.3 us
    dot_general x1, matrix products, body(): jnp.dot(phase_left, coupling_low, preferred_element_type=jnp.float32)  8.07 us
    dot_general x1, matrix products, body(): jnp.dot(phase_right.T, orbitals, preferred_element_type=jnp.float32)  7.94 us
    dot_general x1, matrix products, body(): jnp.dot(full_wide, cross_scaled, precision=lax.Precision.HIGHEST)  7.69 us
    dot_general x1, matrix products, body(): jnp.dot(image, intersection_scaled.T, precision=lax.Precision.HIGHEST)  7.16 us
  transfers between devices with their start and end apart: 5, of which 2 were waited for; matrix products, arithmetic and copies ran while one was open for 9% of the time, Pallas kernels for 0%

commit v1 on v0

v1 whole, which is shorter than its diff:
```python
import math

import jax
import jax.numpy as jnp
from jax import lax
from jax.sharding import PartitionSpec as P

REACH = 2
F32 = jnp.float32
BF16 = jnp.bfloat16
F16 = jnp.float16


def split(value):
    high = lax.reduce_precision(value, 8, 7)
    return high.astype(BF16), (value - high).astype(BF16)


def dot_t(a, b):
    return lax.dot_general(a, b, (((0,), (0,)), ((), ())), preferred_element_type=F32)


def dot(a, b):
    return jnp.dot(a, b, preferred_element_type=F32)


class Cube:
    def __init__(self, chips, cores):
        count = chips.bit_length() - 1
        first = list(range(count))
        second = list(range(count))
        if count >= 3:
            first[1], first[2] = 2, 1
        if count >= 2:
            second[0], second[1] = 1, 0
        orders = (first, second)
        me = lax.axis_index("wire")
        core = lax.axis_index("col") % 2
        self.steps = []
        for k in range(count):
            perm = []
            for w in range(chips):
                for c in range(cores):
                    perm.append((w * cores + c, (w ^ (1 << orders[c % 2][k])) * cores + c))
            bit = (me >> jnp.where(core == 0, first[k], second[k])) & 1
            self.steps.append((perm, bit))

    def send(self, value, k):
        return lax.ppermute(value, ("wire", "col"), self.steps[k][0])

    def scatter(self, value, wire_type, steps):
        for k in steps:
            bit = self.steps[k][1]
            half = value.shape[0] // 2
            out = lax.dynamic_slice_in_dim(value, (1 - bit) * half, half, 0).astype(wire_type)
            got = self.send(out, k)
            value = lax.dynamic_slice_in_dim(value, bit * half, half, 0) + got.astype(F32)
        return value

    def gather(self, value, steps):
        for k in reversed(steps):
            bit = self.steps[k][1]
            got = self.send(value, k)
            value = jnp.where(
                bit == 0,
                jnp.concatenate([value, got], axis=0),
                jnp.concatenate([got, value], axis=0),
            )
        return value


def body(hamiltonian, offsets, phase_left, phase_right, orbitals):
    local_blocks = hamiltonian.shape[0]
    block_size = hamiltonian.shape[2]
    local_rows, cols = orbitals.shape
    rank = phase_left.shape[1]
    chips = lax.axis_size("wire")
    cores = lax.axis_size("col")
    total_rows = local_rows * chips
    cube = Cube(chips, cores)
    steps = list(range(len(cube.steps)))
    swap = [(i, (i + 1) % cores) for i in range(cores)]

    scale = 2.0 ** -max(0, math.ceil(math.log2(36.0 * total_rows / 32768.0)))
    coupling_part = dot_t(phase_right, orbitals)
    other = lax.ppermute(orbitals, "col", swap)
    own_part = dot_t(orbitals, orbitals) * scale
    other_part = dot_t(other, orbitals) * scale
    stacked = jnp.concatenate([coupling_part, own_part, other_part], axis=0)
    mine = cube.scatter(stacked, F16, steps)

    width = REACH * block_size
    up = [(i, (i + 1) % chips) for i in range(chips)]
    down = [(j, i) for i, j in up]
    before = lax.ppermute(orbitals[local_rows - width :], "wire", up)
    after = lax.ppermute(orbitals[:width], "wire", down)
    padded = jnp.concatenate([before, orbitals, after], axis=0)
    tiles = padded.reshape(local_blocks + 2 * REACH, block_size, cols)
    picks = jnp.arange(local_blocks, dtype=jnp.int32)[:, None] + offsets + REACH
    picked = jnp.take(tiles, picks, axis=0)
    band = jnp.einsum(
        "jsab,jsbm->jam", hamiltonian, picked, preferred_element_type=F32
    ).reshape(local_rows, cols)
    full = jnp.concatenate([orbitals, other], axis=1)
    band_high, band_low = split(band)
    cross_band = dot_t(full, band_high) + dot_t(full, band_low)
    left_high, left_low = split(dot_t(full, phase_left))

    piece = mine.shape[0]
    start = jnp.int32(0)
    span = stacked.shape[0]
    for _, bit in cube.steps:
        span //= 2
        start = start + bit * span
    row = start + lax.broadcasted_iota(jnp.int32, (piece, 1), 0)
    mine = jnp.where(row < rank, lax.reduce_precision(mine, 8, 7), mine).astype(F16)
    whole = cube.gather(mine, steps)
    coupling = whole[:rank].astype(BF16)
    inter_own = whole[rank : rank + cols].astype(F32) * (1.0 / (scale * total_rows))
    inter_other = whole[rank + cols :].astype(F32) * (1.0 / (scale * total_rows))

    cross_part = cross_band + dot(left_high, coupling) + dot(left_low, coupling)
    cross = cube.gather(cube.scatter(cross_part, F32, steps), steps) * (1.0 / total_rows)

    image = band + dot(phase_left, coupling)
    image_other = lax.ppermute(image, "col", swap)
    image_high, image_low = split(image)
    other_high, other_low = split(image_other)
    own_high, own_low = split(inter_own)
    cross_high, cross_low = split(inter_other)
    mixed = (
        dot(image_high, own_high)
        + dot(image_low, own_high)
        + dot(image_high, own_low)
        + dot(other_high, cross_high)
        + dot(other_low, cross_high)
        + dot(other_high, cross_low)
    )
    first = 2.0 * image - mixed
    high, low = split(cross)
    return first - (dot(full, high) + dot(full, low))


def solution(mesh):
    return jax.shard_map(
        body,
        mesh=mesh,
        in_specs=(
            P("wire", None, None, None),
            P("wire", None),
            P("wire", None),
            P("wire", None),
            P("wire", "col"),
        ),
        out_specs=P("wire", "col"),
        check_vma=False,
    )
```

time: 297 us -> 139 us (0.47)
  blocking collectives: 99.8 us -> 0 us
  waiting for transfers between devices: 123 us -> 46.3 us
  starting transfers between devices: 7.34 us -> 36.1 us
  between operations: 13.2 us -> 0.41 us
  matrix products: 43.1 us -> 35.2 us
  local copies, waits for them, and re-layouts: 9.57 us -> 15.6 us
  other arithmetic: 1.34 us -> 4.61 us
    psum x1 -> x0, waiting for transfers between devices: 110 us -> none  [body(): lax.psum((coupling_part, intersection_part), 'wire')]
    psum x1 -> x0, blocking collectives: 99.8 us -> none  [body(): lax.psum((coupling_part, intersection_part), 'wire')]
    ppermute x2 -> x20, waiting for transfers between devices: 0.01 us -> 46.3 us  [the longest x16 46.3 us: send(): return lax.ppermute(value, ('wire', 'col'), self.steps[k][0])]
    ppermute x2 -> x20, starting transfers between devices: 7.08 us -> 36.1 us  [the longest x16 31 us: send(): return lax.ppermute(value, ('wire', 'col'), self.steps[k][0])]
    reduce_scatter x1 -> x0, waiting for transfers between devices: 11.3 us -> none  [body(): lax.psum_scatter(partial_terms, 'col', scatter_dimension=1, tiled=True)]
    dot_general x6 -> x17, matrix products: 39 us -> 32.4 us  [the longest x6 18.2 us: dot_t(): lax.dot_general(a, b, (((0,), (0,)), ((), ())), preferred_element_type=F32)]
    unnamed x10 -> x29, local copies, waits for them, and re-layouts: 0.02 us -> 3.99 us
  transfers between devices with their start and end apart: 5 -> 20, of which waited for: 2 -> 15; matrix products, arithmetic and copies ran while one was open for 9% -> 30% of each run, Pallas kernels for 0% -> 0%
where the time goes in v1:
time: 139 us; the launch traced here: 138 us
  waiting for transfers between devices  46.3 us (33%)
  starting transfers between devices  36.1 us (26%)
  matrix products  35.2 us (25%)
  local copies, waits for them, and re-layouts  15.6 us (11%)
  other arithmetic  4.61 us (3%)
    ppermute x16, waiting for transfers between devices, send(): return lax.ppermute(value, ('wire', 'col'), self.steps[k][0])  46.3 us
    ppermute x16, starting transfers between devices, send(): return lax.ppermute(value, ('wire', 'col'), self.steps[k][0])  31 us
    dot_general x6, matrix products, dot_t(): lax.dot_general(a, b, (((0,), (0,)), ((), ())), preferred_element_type=F32)  18.2 us
    dot_general x11, matrix products, dot(): return jnp.dot(a, b, preferred_element_type=F32)  14.2 us
    ppermute x1, starting transfers between devices, body(): after = lax.ppermute(orbitals[:width], 'wire', down)  4.53 us
    unnamed x29, local copies, waits for them, and re-layouts  3.99 us
    gather x1, local copies, waits for them, and re-layouts, body(): picked = jnp.take(tiles, picks, axis=0)  3.8 us
    sub x1, local copies, waits for them, and re-layouts, body(): return first - (dot(full, high) + dot(full, low))  2.88 us
  transfers between devices with their start and end apart: 20, of which 15 were waited for; matrix products, arithmetic and copies ran while one was open for 30% of the time, Pallas kernels for 0%

profile of v1, /device:TPU:0, one launch (start us, length us, event | category | flops | bytes accessed | tf_op | source)
XLA Modules:
  0.0 138.3 jit_solution(3512024831569343693)
XLA Ops:
  0.0 0.5 collective-permute-start.2
  0.5 2.1 %convolution_multiply_fusion.1 = f32[256,256]{1,0:T(8,128)S(1)} fusion(bf16[2048,256]{1,0:T(8,128)(2,1)} %param.9), kind=kOutput, calls=%fused_computation.38 | convolution fusion | flops 268500992 | bytes 1310720 | tf_op jit(solution)/shard_map/dot_general | solution.py:20
  2.6 6.0 %fusion.54 = f32[2048,256]{1,0:T(8,128)S(1)} fusion(bf16[2048,2048]{1,0:T(8,128)(2,1)} %param.8, bf16[2048,256]{1,0:T(8,128)(2,1)S(1)} %copy-done.5), kind=kOutput, calls=%fused_computation.105 | convolution fusion | flops 2147483648 | bytes 11534336 | tf_op jit(solution)/shard_map/dot_general | solution.py:20
  8.6 1.7 %convolution_multiply_fusion = f32[256,256]{1,0:T(8,128)S(1)} fusion(bf16[2048,256]{1,0:T(8,128)(2,1)} %collective-permute-done.2, bf16[2048,256]{1,0:T(8,128)(2,1)S(1)} %copy-done.5), kind=kOutput, calls=%fused_computation.37 | convolution fusion | flops 268500992 | bytes 2359296 | tf_op jit(solution)/shard_map/dot_general | solution.py:20
  10.3 0.2 pad_maximum_fusion
  10.5 1.5 %copy-done.10 = f32[2560,256]{1,0:T(8,128)} copy-done((f32[2560,256]{1,0:T(8,128)}, f32[2560,256]{1,0:T(8,128)S(1)}, u32[]{:S(2)}) %copy-start.10) | copy-done | bytes 2621464
  12.1 2.6 %collective-permute-start.3 = (f16[1280,256]{1,0:T(8,128)(2,1)S(1)}, f16[1280,256]{1,0:T(8,128)(2,1)}, u32[]{:S(2)}, u32[]{:S(2)}) collective-permute-start(f16[1280,256]{1,0:T(8,128)(2,1)S(1)} %dynamic-slice_convert_fusion), channel_id=1, source_target_pairs={{0,2},{1,5},{2,0},{3,7},{4,6},{5,1},{6,4},{7,3},{8,10},{9,13},{10,... | collective-permute-start | bytes 1966088 | tf_op jit(solution)/shard_map/ppermute | solution.py:49
  14.8 0.7 fusion.53
  15.5 4.5 %collective-permute-start.1 = (bf16[256,256]{1,0:T(8,128)(2,1)}, bf16[256,256]{1,0:T(8,128)(2,1)S(1)}, u32[]{:S(2)}, u32[]{:S(2)}) collective-permute-start(bf16[256,256]{1,0:T(8,128)(2,1)} %get-tuple-element.6), channel_id=1, source_target_pairs={{2,0},{4,2},{6,4},{8,6},{10,8},{12,10},{14,12},{16,14},{18,16},{20... | collective-permute-start | bytes 393224 | tf_op jit(solution)/shard_map/ppermute | solution.py:96
  20.0 7.0 %collective-permute-done.3 = f16[1280,256]{1,0:T(8,128)(2,1)} collective-permute-done((f16[1280,256]{1,0:T(8,128)(2,1)S(1)}, f16[1280,256]{1,0:T(8,128)(2,1)}, u32[]{:S(2)}, u32[]{:S(2)}) %collective-permute-start.3) | collective-permute-done | bytes 655392 | tf_op jit(solution)/shard_map/ppermute | solution.py:49
  27.1 1.7 %convert_add_fusion = f32[1280,256]{1,0:T(8,128)S(1)} fusion(f16[1280,256]{1,0:T(8,128)(2,1)} %collective-permute-done.3, f32[2560,256]{1,0:T(8,128)} %copy-done.10, s32[]{:T(128)S(6)} %select_n.153), kind=kLoop, calls=%fused_computation.32 | loop fusion | flops 655360 | bytes 3276804 | tf_op jit(solution)/shard_map/add | solution.py:57
  28.7 1.1 copy-done.11
  29.9 1.6 %collective-permute-start.4 = (f16[640,256]{1,0:T(8,128)(2,1)S(1)}, f16[640,256]{1,0:T(8,128)(2,1)S(1)}, u32[]{:S(2)}, u32[]{:S(2)}) collective-permute-start(f16[640,256]{1,0:T(8,128)(2,1)S(1)} %dynamic-slice_convert_fusion.1), channel_id=1, source_target_pairs={{0,8},{1,3},{2,10},{3,1},{4,12},{5,7},{6,14},{7,5},{8,0},{9,11},{1... | collective-permute-start | bytes 983048 | tf_op jit(solution)/shard_map/ppermute | solution.py:49
  31.7 1.0 constant_dynamic-update-slice_fusion.1
  32.7 4.3 %collective-permute-done.4 = f16[640,256]{1,0:T(8,128)(2,1)S(1)} collective-permute-done((f16[640,256]{1,0:T(8,128)(2,1)S(1)}, f16[640,256]{1,0:T(8,128)(2,1)S(1)}, u32[]{:S(2)}, u32[]{:S(2)}) %collective-permute-start.4) | collective-permute-done | bytes 327712 | tf_op jit(solution)/shard_map/ppermute | solution.py:49
  37.1 2.2 %collective-permute-start.5 = (f16[320,256]{1,0:T(8,128)(2,1)S(1)}, f16[320,256]{1,0:T(8,128)(2,1)S(1)}, u32[]{:S(2)}, u32[]{:S(2)}) collective-permute-start(f16[320,256]{1,0:T(8,128)(2,1)S(1)} %dynamic-slice_convert_fusion.2), channel_id=1, source_target_pairs={{0,4},{1,9},{2,6},{3,11},{4,0},{5,13},{6,2},{7,15},{8,12},{9,1},{1... | collective-permute-start | bytes 491528 | tf_op jit(solution)/shard_map/ppermute | solution.py:49
  39.4 3.3 %collective-permute-done.5 = f16[320,256]{1,0:T(8,128)(2,1)S(1)} collective-permute-done((f16[320,256]{1,0:T(8,128)(2,1)S(1)}, f16[320,256]{1,0:T(8,128)(2,1)S(1)}, u32[]{:S(2)}, u32[]{:S(2)}) %collective-permute-start.5) | collective-permute-done | bytes 163872 | tf_op jit(solution)/shard_map/ppermute | solution.py:49
  42.7 3.3 %collective-permute-start.6 = (f16[160,256]{1,0:T(8,128)(2,1)S(1)}, f16[160,256]{1,0:T(8,128)(2,1)S(1)}, u32[]{:S(2)}, u32[]{:S(2)}) collective-permute-start(f16[160,256]{1,0:T(8,128)(2,1)S(1)} %dynamic-slice_convert_fusion.3), channel_id=1, source_target_pairs={{0,16},{1,17},{2,18},{3,19},{4,20},{5,21},{6,22},{7,23},{8,24},{9,... | collective-permute-start | bytes 245768 | tf_op jit(solution)/shard_map/ppermute | solution.py:49
  46.1 4.9 %collective-permute-done.6 = f16[160,256]{1,0:T(8,128)(2,1)S(1)} collective-permute-done((f16[160,256]{1,0:T(8,128)(2,1)S(1)}, f16[160,256]{1,0:T(8,128)(2,1)S(1)}, u32[]{:S(2)}, u32[]{:S(2)}) %collective-permute-start.6) | collective-permute-done | bytes 81952 | tf_op jit(solution)/shard_map/ppermute | solution.py:49
  51.1 1.3 collective-permute-start.7
  52.5 4.0 %collective-permute-done.7 = f16[160,256]{1,0:T(8,128)(2,1)S(1)} collective-permute-done((f16[160,256]{1,0:T(8,128)(2,1)S(1)}, f16[160,256]{1,0:T(8,128)(2,1)S(1)}, u32[]{:S(2)}, u32[]{:S(2)}) %collective-permute-start.7) | collective-permute-done | bytes 81952 | tf_op jit(solution)/shard_map/ppermute | solution.py:49
  56.6 0.2 collective-permute-start.8
  56.7 1.2 pad_maximum_fusion.1
  57.9 3.8 %gather_fusion = bf16[48,128,256]{2,1,0:T(8,128)(2,1)} fusion(bf16[20,128,256]{2,1,0:T(8,128)(2,1)} %bitcast.29, s32[1024]{0:T(1024)S(1)} %pad_clamp_fusion), kind=kCustom, calls=%fused_computation | custom fusion | bytes 6291648 | tf_op jit(solution)/shard_map/jit(_take)/gather | solution.py:100
  61.7 0.2 collective-permute-done.8
  62.1 3.5 %collective-permute-start.9 = (f16[640,256]{1,0:T(8,128)(2,1)S(1)}, f16[640,256]{1,0:T(8,128)(2,1)S(1)}, u32[]{:S(2)}, u32[]{:S(2)}) collective-permute-start(f16[640,256]{1,0:T(8,128)(2,1)S(1)} %maximum_select_fusion.3), channel_id=1, source_target_pairs={{0,8},{1,3},{2,10},{3,1},{4,12},{5,7},{6,14},{7,5},{8,0},{9,11},{1... | collective-permute-start | bytes 983048 | tf_op jit(solution)/shard_map/ppermute | solution.py:49
  65.6 2.9 %fusion.1 = f32[16,256,128,1]{1,2,3,0:T(8,128)S(1)} fusion(bf16[16,3,128,128]{3,2,1,0:T(8,128)(2,1)S(1)} %copy-done, bf16[16,3,128,256]{3,2,1,0:T(8,128)(2,1)} %bitcast.30, pred[16,3]{1,0:T(8,128)(4,1)S(1)} %copy.18), kind=kOutput, calls=%fused_computation.4 | convolution fusion | flops 404226048 | bytes 6815792 | tf_op jit(solution)/shard_map/jsab,jsbm->jam/dot_general | solution.py:101
  68.5 2.1 %constant_dynamic-update-slice_fusion = bf16[2048,512]{1,0:T(8,128)(2,1)S(1)} fusion(bf16[2048,512]{1,0:T(8,128)(2,1)S(1)} %copy-done.2, bf16[2048,256]{1,0:T(8,128)(2,1)} %collective-permute-done.2), kind=kLoop, calls=%fused_computation.85 | loop fusion | bytes 2097152 | tf_op jit(solution)/shard_map/concatenate | solution.py:104
  70.7 0.3 maximum_select_fusion.1
  71.0 1.9 %collective-permute-start.10 = (f16[1280,256]{1,0:T(8,128)(2,1)S(1)}, f16[1280,256]{1,0:T(8,128)(2,1)S(1)}, u32[]{:S(2)}, u32[]{:S(2)}) collective-permute-start(f16[1280,256]{1,0:T(8,128)(2,1)S(1)} %maximum_select_fusion.1), channel_id=1, source_target_pairs={{0,2},{1,5},{2,0},{3,7},{4,6},{5,1},{6,4},{7,3},{8,10},{9,13},{10,... | collective-permute-start | bytes 1966088 | tf_op jit(solution)/shard_map/ppermute | solution.py:49
  72.8 6.9 %fusion.55 = f32[512,2048]{1,0:T(8,128)S(1)} fusion(bf16[2048,512]{1,0:T(8,128)(2,1)S(1)} %constant_dynamic-update-slice_fusion, bf16[2048,2048]{1,0:T(8,128)(2,1)} %param.7), kind=kOutput, calls=%fused_computation.106 | convolution fusion | flops 4294967296 | bytes 14680064 | tf_op jit(solution)/shard_map/dot_general | solution.py:20
  79.7 0.7 fusion.18
  80.5 1.1 collective-permute-done.10
  81.6 0.6 maximum_select_fusion
  82.2 0.7 fusion.12
  82.9 0.3 copy-done.8
  83.2 0.7 fusion.14
  84.0 0.8 fusion.17
  84.8 1.9 %collective-permute-start.12 = (f32[256,256]{1,0:T(8,128)S(1)}, f32[256,256]{1,0:T(8,128)S(1)}, u32[]{:S(2)}, u32[]{:S(2)}) collective-permute-start(f32[256,256]{1,0:T(8,128)S(1)} %constant_dynamic-slice_fusion.3), channel_id=1, source_target_pairs={{0,2},{1,5},{2,0},{3,7},{4,6},{5,1},{6,4},{7,3},{8,10},{9,13},{10,... | collective-permute-start | bytes 786440 | tf_op jit(solution)/shard_map/ppermute | solution.py:49
  86.7 4.6 %collective-permute-done.12 = f32[256,256]{1,0:T(8,128)S(1)} collective-permute-done((f32[256,256]{1,0:T(8,128)S(1)}, f32[256,256]{1,0:T(8,128)S(1)}, u32[]{:S(2)}, u32[]{:S(2)}) %collective-permute-start.12) | collective-permute-done | bytes 262176 | tf_op jit(solution)/shard_map/ppermute | solution.py:49
  91.3 2.1 %collective-permute-start.13 = (f32[128,256]{1,0:T(8,128)S(1)}, f32[128,256]{1,0:T(8,128)S(1)}, u32[]{:S(2)}, u32[]{:S(2)}) collective-permute-start(f32[128,256]{1,0:T(8,128)S(1)} %constant_dynamic-slice_fusion.2), channel_id=1, source_target_pairs={{0,8},{1,3},{2,10},{3,1},{4,12},{5,7},{6,14},{7,5},{8,0},{9,11},{1... | collective-permute-start | bytes 393224 | tf_op jit(solution)/shard_map/ppermute | solution.py:49
  93.4 2.9 %collective-permute-done.13 = f32[128,256]{1,0:T(8,128)S(1)} collective-permute-done((f32[128,256]{1,0:T(8,128)S(1)}, f32[128,256]{1,0:T(8,128)S(1)}, u32[]{:S(2)}, u32[]{:S(2)}) %collective-permute-start.13) | collective-permute-done | bytes 131104 | tf_op jit(solution)/shard_map/ppermute | solution.py:49
  96.4 1.5 %collective-permute-start.14 = (f32[64,256]{1,0:T(8,128)S(1)}, f32[64,256]{1,0:T(8,128)S(1)}, u32[]{:S(2)}, u32[]{:S(2)}) collective-permute-start(f32[64,256]{1,0:T(8,128)S(1)} %constant_dynamic-slice_fusion.1), channel_id=1, source_target_pairs={{0,4},{1,9},{2,6},{3,11},{4,0},{5,13},{6,2},{7,15},{8,12},{9,1},{1... | collective-permute-start | bytes 196616 | tf_op jit(solution)/shard_map/ppermute | solution.py:49
  97.9 2.8 %collective-permute-done.14 = f32[64,256]{1,0:T(8,128)S(1)} collective-permute-done((f32[64,256]{1,0:T(8,128)S(1)}, f32[64,256]{1,0:T(8,128)S(1)}, u32[]{:S(2)}, u32[]{:S(2)}) %collective-permute-start.14) | collective-permute-done | bytes 65568 | tf_op jit(solution)/shard_map/ppermute | solution.py:49
  100.7 2.5 %collective-permute-start.15 = (f32[32,256]{1,0:T(8,128)S(1)}, f32[32,256]{1,0:T(8,128)S(1)}, u32[]{:S(2)}, u32[]{:S(2)}) collective-permute-start(f32[32,256]{1,0:T(8,128)S(1)} %constant_dynamic-slice_fusion), channel_id=1, source_target_pairs={{0,16},{1,17},{2,18},{3,19},{4,20},{5,21},{6,22},{7,23},{8,24},{9,... | collective-permute-start | bytes 98312 | tf_op jit(solution)/shard_map/ppermute | solution.py:49
  103.2 1.8 %copy.20 = f32[2048,256]{0,1:T(8,128)} copy(f32[2048,256]{1,0:T(8,128)S(1)} %bitcast.28) | data formatting | bytes 4194304 | tf_op jit(solution)/shard_map/reshape | solution.py:103
  105.0 0.6 collective-permute-done.15
  105.6 2.5 %collective-permute-start.16 = (f32[32,256]{1,0:T(8,128)S(1)}, f32[32,256]{1,0:T(8,128)S(1)}, u32[]{:S(2)}, u32[]{:S(2)}) collective-permute-start(f32[32,256]{1,0:T(8,128)S(1)} %dynamic-slice_add_fusion.3), channel_id=1, source_target_pairs={{0,16},{1,17},{2,18},{3,19},{4,20},{5,21},{6,22},{7,23},{8,24},{9,... | collective-permute-start | bytes 98312 | tf_op jit(solution)/shard_map/ppermute | solution.py:49
  108.1 6.7 %fusion.8 = f32[2048,256]{0,1:T(8,128)S(1)} fusion(f32[2048,256]{0,1:T(8,128)} %copy.20, bf16[2048,2048]{1,0:T(8,128)(2,1)} %param.7, f16[2560,256]{1,0:T(8,128)(2,1)} %copy-done.8), kind=kOutput, calls=%fused_computation.23 | convolution fusion | flops 2148532224 | bytes 13631488 | tf_op jit(solution)/shard_map/dot_general | solution.py:24
  114.9 0.2 collective-permute-start.17
  115.1 0.5 fusion.25
  115.6 3.6 %collective-permute-done.17 = f32[64,256]{1,0:T(8,128)S(1)} collective-permute-done((f32[64,256]{1,0:T(8,128)S(1)}, f32[64,256]{1,0:T(8,128)S(1)}, u32[]{:S(2)}, u32[]{:S(2)}) %collective-permute-start.17) | collective-permute-done | bytes 65568 | tf_op jit(solution)/shard_map/ppermute | solution.py:49
  119.2 2.1 %collective-permute-start.18 = (f32[128,256]{1,0:T(8,128)S(1)}, f32[128,256]{1,0:T(8,128)S(1)}, u32[]{:S(2)}, u32[]{:S(2)}) collective-permute-start(f32[128,256]{1,0:T(8,128)S(1)} %maximum_select_fusion.6), channel_id=1, source_target_pairs={{0,8},{1,3},{2,10},{3,1},{4,12},{5,7},{6,14},{7,5},{8,0},{9,11},{1... | collective-permute-start | bytes 393224 | tf_op jit(solution)/shard_map/ppermute | solution.py:49
  121.3 0.5 convolution_add_fusion.3
  121.8 2.4 %collective-permute-done.18 = f32[128,256]{1,0:T(8,128)S(1)} collective-permute-done((f32[128,256]{1,0:T(8,128)S(1)}, f32[128,256]{1,0:T(8,128)S(1)}, u32[]{:S(2)}, u32[]{:S(2)}) %collective-permute-start.18) | collective-permute-done | bytes 131104 | tf_op jit(solution)/shard_map/ppermute | solution.py:49
  124.3 1.5 %collective-permute-start.19 = (f32[256,256]{1,0:T(8,128)S(1)}, f32[256,256]{1,0:T(8,128)S(1)}, u32[]{:S(2)}, u32[]{:S(2)}) collective-permute-start(f32[256,256]{1,0:T(8,128)S(1)} %maximum_select_fusion.4), channel_id=1, source_target_pairs={{0,2},{1,5},{2,0},{3,7},{4,6},{5,1},{6,4},{7,3},{8,10},{9,13},{10,... | collective-permute-start | bytes 786440 | tf_op jit(solution)/shard_map/ppermute | solution.py:49
  125.8 0.5 convolution_add_fusion.2
  126.4 4.4 %collective-permute-done.19 = f32[256,256]{1,0:T(8,128)S(1)} collective-permute-done((f32[256,256]{1,0:T(8,128)S(1)}, f32[256,256]{1,0:T(8,128)S(1)}, u32[]{:S(2)}, u32[]{:S(2)}) %collective-permute-start.19) | collective-permute-done | bytes 262176 | tf_op jit(solution)/shard_map/ppermute | solution.py:49
  130.7 0.8 fusion.29
  131.5 0.8 convolution_add_fusion
  132.3 0.5 fusion.26
  132.8 0.5 fusion.20
  133.3 2.1 %fusion.7 = f32[2048,256]{0,1:T(8,128)} fusion(f32[2048,256]{0,1:T(8,128)S(1)} %convolution_add_fusion, f32[2048,256]{0,1:T(8,128)S(1)} %fusion.26, f32[2048,256]{0,1:T(8,128)S(1)} %fusion.20, f32[2048,256]{0,1:T(8,128)S(1)} %convolution_add_fusion.2, f32[2048,256]{0,1:T(8,128)S(1)} %fusion.8, f32[2048,256]{0,1:T(8,128)S(1)} %collective-permute-done.11, ...), kind=kOutput, calls=%fused_computation.19 | convolution fusion | flops 272891904 | bytes 14811136 | tf_op jit(solution)/shard_map/dot_general | solution.py:24
  135.4 2.9 %copy.29 = f32[2048,256]{1,0:T(8,128)} copy(f32[2048,256]{0,1:T(8,128)} %fusion.7) | data formatting | bytes 4194304 | tf_op jit(solution)/shard_map/sub | solution.py:141
  (60 shorter events, 1.4 us)
Async XLA Ops:
  0.0 65.6 %copy-start = (bf16[16,3,128,128]{3,2,1,0:T(8,128)(2,1)S(1)}, bf16[16,3,128,128]{3,2,1,0:T(8,128)(2,1)}, u32[]{:S(2)}) copy-start(bf16[16,3,128,128]{3,2,1,0:T(8,128)(2,1)} %param.5) | copy-start | bytes 4718596
  0.0 2.6 %copy-start.5 = (bf16[2048,256]{1,0:T(8,128)(2,1)S(1)}, bf16[2048,256]{1,0:T(8,128)(2,1)}, u32[]{:S(2)}) copy-start(bf16[2048,256]{1,0:T(8,128)(2,1)} %param.9) | copy-start | bytes 3145732
  0.0 8.6 %collective-permute-start.2 = (bf16[2048,256]{1,0:T(8,128)(2,1)}, bf16[2048,256]{1,0:T(8,128)(2,1)}, u32[]{:S(2)}, u32[]{:S(2)}) collective-permute-start(bf16[2048,256]{1,0:T(8,128)(2,1)} %param.9), channel_id=1, source_target_pairs={{0,1},{1,0},{2,3},{3,2},{4,5},{5,4},{6,7},{7,6},{8,9},{9,8},{10,11... | collective-permute-start | bytes 3145736 | tf_op jit(solution)/shard_map/ppermute | solution.py:86
  10.5 1.5 %copy-start.10 = (f32[2560,256]{1,0:T(8,128)}, f32[2560,256]{1,0:T(8,128)S(1)}, u32[]{:S(2)}) copy-start(f32[2560,256]{1,0:T(8,128)S(1)} %pad_maximum_fusion) | copy-start | bytes 7864324
  12.1 15.0 %collective-permute-start.3 = (f16[1280,256]{1,0:T(8,128)(2,1)S(1)}, f16[1280,256]{1,0:T(8,128)(2,1)}, u32[]{:S(2)}, u32[]{:S(2)}) collective-permute-start(f16[1280,256]{1,0:T(8,128)(2,1)S(1)} %dynamic-slice_convert_fusion), channel_id=1, source_target_pairs={{0,2},{1,5},{2,0},{3,7},{4,6},{5,1},{6,4},{7,3},{8,10},{9,13},{10,... | collective-permute-start | bytes 1966088 | tf_op jit(solution)/shard_map/ppermute | solution.py:49
  15.5 41.2 %collective-permute-start.1 = (bf16[256,256]{1,0:T(8,128)(2,1)}, bf16[256,256]{1,0:T(8,128)(2,1)S(1)}, u32[]{:S(2)}, u32[]{:S(2)}) collective-permute-start(bf16[256,256]{1,0:T(8,128)(2,1)} %get-tuple-element.6), channel_id=1, source_target_pairs={{2,0},{4,2},{6,4},{8,6},{10,8},{12,10},{14,12},{16,14},{18,16},{20... | collective-permute-start | bytes 393224 | tf_op jit(solution)/shard_map/ppermute | solution.py:96
  20.0 36.7 %collective-permute-start = (bf16[256,256]{1,0:T(8,128)(2,1)}, bf16[256,256]{1,0:T(8,128)(2,1)S(1)}, u32[]{:S(2)}, u32[]{:S(2)}) collective-permute-start(bf16[256,256]{1,0:T(8,128)(2,1)} %get-tuple-element.5), channel_id=1, source_target_pairs={{0,2},{2,4},{4,6},{6,8},{8,10},{10,12},{12,14},{14,16},{16,18},{18... | collective-permute-start | bytes 393224 | tf_op jit(solution)/shard_map/ppermute | solution.py:95
  20.0 11.5 %copy-start.13 = (s32[16,3]{0,1:T(4,128)S(1)}, s32[16,3]{0,1:T(4,128)}, u32[]{:S(2)}) copy-start(s32[16,3]{0,1:T(4,128)} %param.6) | copy-start | bytes 580
  28.7 1.1 copy-start.11
  29.9 7.1 %collective-permute-start.4 = (f16[640,256]{1,0:T(8,128)(2,1)S(1)}, f16[640,256]{1,0:T(8,128)(2,1)S(1)}, u32[]{:S(2)}, u32[]{:S(2)}) collective-permute-start(f16[640,256]{1,0:T(8,128)(2,1)S(1)} %dynamic-slice_convert_fusion.1), channel_id=1, source_target_pairs={{0,8},{1,3},{2,10},{3,1},{4,12},{5,7},{6,14},{7,5},{8,0},{9,11},{1... | collective-permute-start | bytes 983048 | tf_op jit(solution)/shard_map/ppermute | solution.py:49
  31.7 5.3 %copy-start.12 = (f32[1280,256]{1,0:T(8,128)S(1)}, f32[1280,256]{1,0:T(8,128)}, u32[]{:S(2)}) copy-start(f32[1280,256]{1,0:T(8,128)} %copy-done.11) | copy-start | bytes 3932164
  37.1 5.5 %collective-permute-start.5 = (f16[320,256]{1,0:T(8,128)(2,1)S(1)}, f16[320,256]{1,0:T(8,128)(2,1)S(1)}, u32[]{:S(2)}, u32[]{:S(2)}) collective-permute-start(f16[320,256]{1,0:T(8,128)(2,1)S(1)} %dynamic-slice_convert_fusion.2), channel_id=1, source_target_pairs={{0,4},{1,9},{2,6},{3,11},{4,0},{5,13},{6,2},{7,15},{8,12},{9,1},{1... | collective-permute-start | bytes 491528 | tf_op jit(solution)/shard_map/ppermute | solution.py:49
  42.7 8.2 %collective-permute-start.6 = (f16[160,256]{1,0:T(8,128)(2,1)S(1)}, f16[160,256]{1,0:T(8,128)(2,1)S(1)}, u32[]{:S(2)}, u32[]{:S(2)}) collective-permute-start(f16[160,256]{1,0:T(8,128)(2,1)S(1)} %dynamic-slice_convert_fusion.3), channel_id=1, source_target_pairs={{0,16},{1,17},{2,18},{3,19},{4,20},{5,21},{6,22},{7,23},{8,24},{9,... | collective-permute-start | bytes 245768 | tf_op jit(solution)/shard_map/ppermute | solution.py:49
  51.1 5.4 %collective-permute-start.7 = (f16[160,256]{1,0:T(8,128)(2,1)S(1)}, f16[160,256]{1,0:T(8,128)(2,1)S(1)}, u32[]{:S(2)}, u32[]{:S(2)}) collective-permute-start(f16[160,256]{1,0:T(8,128)(2,1)S(1)} %fusion.35), channel_id=1, source_target_pairs={{0,16},{1,17},{2,18},{3,19},{4,20},{5,21},{6,22},{7,23},{8,24},{9,... | collective-permute-start | bytes 245768 | tf_op jit(solution)/shard_map/ppermute | solution.py:49
  56.6 5.4 %collective-permute-start.8 = (f16[320,256]{1,0:T(8,128)(2,1)S(1)}, f16[320,256]{1,0:T(8,128)(2,1)S(1)}, u32[]{:S(2)}, u32[]{:S(2)}) collective-permute-start(f16[320,256]{1,0:T(8,128)(2,1)S(1)} %maximum_select_fusion.5), channel_id=1, source_target_pairs={{0,4},{1,9},{2,6},{3,11},{4,0},{5,13},{6,2},{7,15},{8,12},{9,1},{1... | collective-permute-start | bytes 491528 | tf_op jit(solution)/shard_map/ppermute | solution.py:49
  62.1 8.6 %collective-permute-start.9 = (f16[640,256]{1,0:T(8,128)(2,1)S(1)}, f16[640,256]{1,0:T(8,128)(2,1)S(1)}, u32[]{:S(2)}, u32[]{:S(2)}) collective-permute-start(f16[640,256]{1,0:T(8,128)(2,1)S(1)} %maximum_select_fusion.3), channel_id=1, source_target_pairs={{0,8},{1,3},{2,10},{3,1},{4,12},{5,7},{6,14},{7,5},{8,0},{9,11},{1... | collective-permute-start | bytes 983048 | tf_op jit(solution)/shard_map/ppermute | solution.py:49
  65.6 2.9 %copy-start.2 = (bf16[2048,512]{1,0:T(8,128)(2,1)S(1)}, bf16[2048,512]{1,0:T(8,128)(2,1)}, u32[]{:S(2)}) copy-start(bf16[2048,512]{1,0:T(8,128)(2,1)} %constant_dynamic-update-slice_fusion.1) | copy-start | bytes 6291460
  68.5 15.5 %copy-start.6 = (f32[16,256,128,1]{1,2,3,0:T(8,128)}, f32[16,256,128,1]{1,2,3,0:T(8,128)S(1)}, u32[]{:S(2)}) copy-start(f32[16,256,128,1]{1,2,3,0:T(8,128)S(1)} %fusion.1) | copy-start | bytes 6291460
  70.6 13.4 %copy-start.3 = (bf16[2048,512]{1,0:T(8,128)(2,1)}, bf16[2048,512]{1,0:T(8,128)(2,1)S(1)}, u32[]{:S(2)}) copy-start(bf16[2048,512]{1,0:T(8,128)(2,1)S(1)} %constant_dynamic-update-slice_fusion) | copy-start | bytes 6291460
  71.0 10.7 %collective-permute-start.10 = (f16[1280,256]{1,0:T(8,128)(2,1)S(1)}, f16[1280,256]{1,0:T(8,128)(2,1)S(1)}, u32[]{:S(2)}, u32[]{:S(2)}) collective-permute-start(f16[1280,256]{1,0:T(8,128)(2,1)S(1)} %maximum_select_fusion.1), channel_id=1, source_target_pairs={{0,2},{1,5},{2,0},{3,7},{4,6},{5,1},{6,4},{7,3},{8,10},{9,13},{10,... | collective-permute-start | bytes 1966088 | tf_op jit(solution)/shard_map/ppermute | solution.py:49
  82.2 1.1 copy-start.8
  84.8 18.5 %copy-start.7 = (f32[16,256,128,1]{1,2,3,0:T(8,128)S(1)}, f32[16,256,128,1]{1,2,3,0:T(8,128)}, u32[]{:S(2)}) copy-start(f32[16,256,128,1]{1,2,3,0:T(8,128)} %copy-done.6) | copy-start | bytes 6291460
  84.8 6.4 %collective-permute-start.12 = (f32[256,256]{1,0:T(8,128)S(1)}, f32[256,256]{1,0:T(8,128)S(1)}, u32[]{:S(2)}, u32[]{:S(2)}) collective-permute-start(f32[256,256]{1,0:T(8,128)S(1)} %constant_dynamic-slice_fusion.3), channel_id=1, source_target_pairs={{0,2},{1,5},{2,0},{3,7},{4,6},{5,1},{6,4},{7,3},{8,10},{9,13},{10,... | collective-permute-start | bytes 786440 | tf_op jit(solution)/shard_map/ppermute | solution.py:49
  91.3 5.0 %collective-permute-start.13 = (f32[128,256]{1,0:T(8,128)S(1)}, f32[128,256]{1,0:T(8,128)S(1)}, u32[]{:S(2)}, u32[]{:S(2)}) collective-permute-start(f32[128,256]{1,0:T(8,128)S(1)} %constant_dynamic-slice_fusion.2), channel_id=1, source_target_pairs={{0,8},{1,3},{2,10},{3,1},{4,12},{5,7},{6,14},{7,5},{8,0},{9,11},{1... | collective-permute-start | bytes 393224 | tf_op jit(solution)/shard_map/ppermute | solution.py:49
  96.4 4.3 %collective-permute-start.14 = (f32[64,256]{1,0:T(8,128)S(1)}, f32[64,256]{1,0:T(8,128)S(1)}, u32[]{:S(2)}, u32[]{:S(2)}) collective-permute-start(f32[64,256]{1,0:T(8,128)S(1)} %constant_dynamic-slice_fusion.1), channel_id=1, source_target_pairs={{0,4},{1,9},{2,6},{3,11},{4,0},{5,13},{6,2},{7,15},{8,12},{9,1},{1... | collective-permute-start | bytes 196616 | tf_op jit(solution)/shard_map/ppermute | solution.py:49
  100.7 4.9 %collective-permute-start.15 = (f32[32,256]{1,0:T(8,128)S(1)}, f32[32,256]{1,0:T(8,128)S(1)}, u32[]{:S(2)}, u32[]{:S(2)}) collective-permute-start(f32[32,256]{1,0:T(8,128)S(1)} %constant_dynamic-slice_fusion), channel_id=1, source_target_pairs={{0,16},{1,17},{2,18},{3,19},{4,20},{5,21},{6,22},{7,23},{8,24},{9,... | collective-permute-start | bytes 98312 | tf_op jit(solution)/shard_map/ppermute | solution.py:49
  105.6 9.5 %copy-start.9 = (f16[2560,256]{1,0:T(8,128)(2,1)S(1)}, f16[2560,256]{1,0:T(8,128)(2,1)}, u32[]{:S(2)}) copy-start(f16[2560,256]{1,0:T(8,128)(2,1)} %copy-done.8) | copy-start | bytes 3932164
  105.6 9.2 %collective-permute-start.16 = (f32[32,256]{1,0:T(8,128)S(1)}, f32[32,256]{1,0:T(8,128)S(1)}, u32[]{:S(2)}, u32[]{:S(2)}) collective-permute-start(f32[32,256]{1,0:T(8,128)S(1)} %dynamic-slice_add_fusion.3), channel_id=1, source_target_pairs={{0,16},{1,17},{2,18},{3,19},{4,20},{5,21},{6,22},{7,23},{8,24},{9,... | collective-permute-start | bytes 98312 | tf_op jit(solution)/shard_map/ppermute | solution.py:49
  114.8 17.5 %collective-permute-start.11 = (f32[2048,256]{0,1:T(8,128)S(1)}, f32[2048,256]{0,1:T(8,128)S(1)}, u32[]{:S(2)}, u32[]{:S(2)}) collective-permute-start(f32[2048,256]{0,1:T(8,128)S(1)} %fusion.8), channel_id=1, source_target_pairs={{0,1},{1,0},{2,3},{3,2},{4,5},{5,4},{6,7},{7,6},{8,9},{9,8},{10,11... | collective-permute-start | bytes 6291464 | tf_op jit(solution)/shard_map/ppermute | solution.py:126
  114.9 4.3 %collective-permute-start.17 = (f32[64,256]{1,0:T(8,128)S(1)}, f32[64,256]{1,0:T(8,128)S(1)}, u32[]{:S(2)}, u32[]{:S(2)}) collective-permute-start(f32[64,256]{1,0:T(8,128)S(1)} %maximum_select_fusion.7), channel_id=1, source_target_pairs={{0,4},{1,9},{2,6},{3,11},{4,0},{5,13},{6,2},{7,15},{8,12},{9,1},{1... | collective-permute-start | bytes 196616 | tf_op jit(solution)/shard_map/ppermute | solution.py:49
  119.2 5.0 %collective-permute-start.18 = (f32[128,256]{1,0:T(8,128)S(1)}, f32[128,256]{1,0:T(8,128)S(1)}, u32[]{:S(2)}, u32[]{:S(2)}) collective-permute-start(f32[128,256]{1,0:T(8,128)S(1)} %maximum_select_fusion.6), channel_id=1, source_target_pairs={{0,8},{1,3},{2,10},{3,1},{4,12},{5,7},{6,14},{7,5},{8,0},{9,11},{1... | collective-permute-start | bytes 393224 | tf_op jit(solution)/shard_map/ppermute | solution.py:49
  124.3 6.5 %copy-start.4 = (bf16[2048,512]{1,0:T(8,128)(2,1)S(1)}, bf16[2048,512]{1,0:T(8,128)(2,1)}, u32[]{:S(2)}) copy-start(bf16[2048,512]{1,0:T(8,128)(2,1)} %copy-done.3) | copy-start | bytes 6291460
  124.3 6.4 %collective-permute-start.19 = (f32[256,256]{1,0:T(8,128)S(1)}, f32[256,256]{1,0:T(8,128)S(1)}, u32[]{:S(2)}, u32[]{:S(2)}) collective-permute-start(f32[256,256]{1,0:T(8,128)S(1)} %maximum_select_fusion.4), channel_id=1, source_target_pairs={{0,2},{1,5},{2,0},{3,7},{4,6},{5,1},{6,4},{7,3},{8,10},{9,13},{10,... | collective-permute-start | bytes 786440 | tf_op jit(solution)/shard_map/ppermute | solution.py:49
  133.3 5.0 %copy-start.1 = (bf16[16,3,128,128]{3,2,1,0:T(8,128)(2,1)S(1)}, bf16[16,3,128,128]{3,2,1,0:T(8,128)(2,1)}, u32[]{:S(2)}) copy-start(bf16[16,3,128,128]{3,2,1,0:T(8,128)(2,1)} %param.5) | copy-start | bytes 4718596
